TPU v7x, 512 devices: a whole 4x8x8 slice. The times are simulated.
512 devices in a mesh: pair: 64 (over z, x, core), slab: 8 (over y).
Axes of the slice: x: 4, y: 8, z: 8, core: 2. Of those that a mesh axis runs over, the one named last changes fastest.
Arguments:
- amps: bfloat16 [1024, 1024, 128], P(('pair', 'slab')), may hold values from -6 to 6
- symmetry: int32 [1024], replicated, may hold values from 0 to 3
- screen: int32 [64, 16, 16], P('pair'), may hold values 0 or 1
- owner: int32 [1024], replicated, may hold values from 0 to 63, as said below
- integrals: bfloat16 [64, 2048, 2048], P('pair', 'slab'), may hold values from -0.25 to 0.25
Outputs:
- residual: bfloat16 [1024, 64, 16, 128], P(('pair', 'slab'))
Inputs may be any that keep to these rules, and one draw needn't show every extreme that they name: Every owner from 0 to 63 holds exactly 16 tiles.
All inputs are finite; a program needn't handle non-finite values. No bound on the sum of `screen` on one device may be relied on, other than what follows from the above.
Results may differ from a plain program's by a relative error of at most 0.001.
Values may be sent and summed in bfloat16 or wider, within the bound.
A program may use at most 64 MiB of HBM per device.

v0:
```python
import jax
import jax.numpy as jnp
from jax import lax
from jax.sharding import PartitionSpec as P


def contract(operand, block_piece, mask_piece, per_owner, tile_width):
    rows_here = block_piece.shape[0]
    masked = (
        block_piece.reshape(rows_here, per_owner, tile_width) * mask_piece[:, :, None]
    ).reshape(rows_here, per_owner * tile_width)
    return jnp.dot(operand, masked, preferred_element_type=jnp.float32)


def on_device(amps, symmetry, screen, owner, integrals):
    n_pair = lax.axis_size("pair")
    local_rows, tile_count, tile_width = amps.shape
    per_owner = tile_count // n_pair
    owner_span = per_owner * tile_width
    tile_order = jnp.argsort(owner, stable=True).reshape(n_pair, per_owner)
    sorted_amps = jnp.take(amps, tile_order.reshape(-1), axis=1).reshape(
        local_rows, n_pair, owner_span
    )
    owned = lax.dynamic_index_in_dim(tile_order, lax.axis_index("pair"), 0, keepdims=False)
    labels = jnp.take(symmetry, owned)
    allowed = ((labels[:, None] == labels[None, :]) & (screen[0] == 1)).astype(jnp.bfloat16)
    mask_rows = jnp.repeat(allowed, tile_width, axis=0)
    block_rows = integrals[0]
    received = lax.all_to_all(sorted_amps, "pair", split_axis=1, concat_axis=1, tiled=True)
    flat_rows = received.reshape(local_rows * n_pair, owner_span)
    summed = contract(
        flat_rows,
        lax.all_gather(block_rows, "slab", axis=0, tiled=True),
        mask_rows,
        per_owner,
        tile_width,
    )
    product = summed.astype(jnp.bfloat16).reshape(local_rows, n_pair, owner_span)
    returned = lax.all_to_all(product, "pair", split_axis=1, concat_axis=1, tiled=True)
    return returned.reshape(local_rows, n_pair, per_owner, tile_width)


def solution(mesh):
    in_specs = (
        P(("pair", "slab"), None, None),
        P(),
        P("pair", None, None),
        P(),
        P("pair", "slab", None),
    )
    out_specs = P(("pair", "slab"), None, None, None)
    return jax.shard_map(
        on_device, mesh=mesh, in_specs=in_specs, out_specs=out_specs, check_vma=False
    )
```

profile of v0, /device:TPU:1, one launch (start us, length us, event | category | flops | bytes accessed | tf_op | source)
XLA Modules:
  0.0 163.3 jit_solution(9701086411608174818)
XLA Ops:
  6.5 0.0 copy-start
  6.5 0.0 copy-start.1
  6.5 0.0 copy-start.2
  6.5 0.0 all-gather.3.cloned.1.call-start
  6.5 0.7 all-gather.3.cloned.1.call-update
  7.3 5.1 %sort.17 = (s32[1024]{0:T(1024)}, s32[1024]{0:T(1024)S(1)}) sort(s32[1024]{0:T(1024)} %param.8, s32[1024]{0:T(1024)S(1)} %iota.4), dimensions={0}, to_apply=%region_0.0 | sort | flops 10240 | bytes 16384 | tf_op jit(solution)/shard_map/jit(argsort)/sort | solution.py:20
  12.3 0.1 broadcast_in_dim.25
  12.4 0.2 broadcast_in_dim.26
  12.6 0.1 copy.23
  12.7 0.0 copy-done
  12.7 4.4 %gather_fusion = bf16[1024,2,128]{2,0,1:T(8,128)(2,1)S(1)} fusion(bf16[2,1024,128]{2,1,0:T(8,128)(2,1)S(1)} %copy-done, s32[1024]{0:T(1024)S(1)} %fusion.5), kind=kCustom, calls=%fused_computation | custom fusion | bytes 1052672 | tf_op jit(solution)/shard_map/jit(_take)/gather | solution.py:21
  17.1 0.2 gather.13
  17.4 1.9 %broadcast_select_fusion = bf16[2,64,2048]{2,0,1:T(2,128)(2,1)} fusion(pred[64,2048]{1,0:T(8,128)(4,1)S(1)} %bitcast.43, bf16[2,64,2048]{2,1,0:T(8,128)(2,1)S(1)} %gather.13), kind=kLoop, calls=%fused_computation.7 | loop fusion | flops 262144 | bytes 1179648 | tf_op jit(solution)/shard_map/jit(_take)/select_n | solution.py:21
  19.2 14.8 %all-to-all-start = ((bf16[2,64,2048]{2,0,1:T(2,128)(2,1)}), bf16[2,64,2048]{2,0,1:T(2,128)(2,1)S(1)}, u32[]{:S(2)}, u32[]{:S(2)}) async-start(bf16[2,64,2048]{2,0,1:T(2,128)(2,1)} %broadcast_select_fusion), calls=%async_computation | async-start | bytes 1048576 | tf_op jit(solution)/shard_map/all_to_all | solution.py:29
  34.1 0.1 reshape.78
  34.2 0.0 copy-done.1
  34.2 0.6 gather_fusion.1
  34.9 0.0 copy-done.2
  34.9 0.1 fusion.4
  35.0 16.8 %all-to-all-done = bf16[2,64,2048]{2,0,1:T(2,128)(2,1)S(1)} async-done(((bf16[2,64,2048]{2,0,1:T(2,128)(2,1)}), bf16[2,64,2048]{2,0,1:T(2,128)(2,1)S(1)}, u32[]{:S(2)}, u32[]{:S(2)}) %all-to-all-start) | async-done | bytes 524320 | tf_op jit(solution)/shard_map/all_to_all | solution.py:29
  51.8 0.2 copy.10
  52.0 59.5 %all-gather.3.cloned.1.call-done = bf16[1,2048,2048]{2,1,0:T(8,128)(2,1)} async-done(((bf16[1,256,2048]{2,1,0:T(8,128)(2,1)}), bf16[1,2048,2048]{2,1,0:T(8,128)(2,1)}) %all-gather.3.cloned.1.call-update) | async-done | bytes 8388624 | tf_op jit(solution)/shard_map/all_gather | solution.py:33
  111.5 0.0 copy-start.3
  111.5 0.1 broadcast_in_dim.31
  111.5 9.0 %mul.14 = bf16[2048,16,128]{2,1,0:T(8,128)(2,1)S(1)} broadcast(bf16[2048,16]{1,0:T(8,128)(2,1)S(1)} %bitcast.41), dimensions={0,1} | broadcast | bytes 8454144 | tf_op jit(solution)/shard_map/mul | solution.py:10
  120.5 0.0 copy-done.3
  120.5 5.7 %fusion.3 = bf16[128,2048]{1,0:T(8,128)(2,1)S(1)} fusion(bf16[128,2048]{1,0:T(8,128)(2,1)S(1)} %bitcast.44, bf16[256,8,16,128]{3,2,1,0:T(8,128)(2,1)S(1)} %bitcast.40, bf16[1,2048,2048]{2,1,0:T(8,128)(2,1)S(1)} %copy-done.3), kind=kOutput, calls=%fused_computation.6 | convolution fusion | flops 1078198272 | bytes 17825792 | tf_op jit(solution)/shard_map/dot_general | solution.py:12
  126.2 0.5 copy.11
  126.7 28.5 %all_to_all.10 = bf16[2,64,2048]{2,0,1:T(2,128)(2,1)S(1)} all-to-all(bf16[2,64,2048]{2,0,1:T(2,128)(2,1)S(1)} %copy.11), channel_id=1, replica_groups=mesh['pair'=64,'slab'=8] {'pair'}, dimensions={1} | all-to-all | bytes 1048576 | tf_op jit(solution)/shard_map/all_to_all | solution.py:39
  155.3 0.3 reshape.80
  155.6 0.8 copy.12
  (7 shorter events, 0.1 us)
Async XLA Ops:
  6.5 6.2 %copy-start = (bf16[2,1024,128]{2,1,0:T(8,128)(2,1)S(1)}, bf16[2,1024,128]{2,1,0:T(8,128)(2,1)}, u32[]{:S(2)}) copy-start(bf16[2,1024,128]{2,1,0:T(8,128)(2,1)} %param.5) | copy-start | bytes 1572868
  6.5 27.7 %copy-start.1 = (s32[1024]{0:T(1024)S(1)}, s32[1024]{0:T(1024)}, u32[]{:S(2)}) copy-start(s32[1024]{0:T(1024)} %param.6) | copy-start | bytes 12292
  6.5 28.3 %copy-start.2 = (s32[1,16,16]{2,1,0:T(8,128)S(1)}, s32[1,16,16]{2,1,0:T(8,128)}, u32[]{:S(2)}) copy-start(s32[1,16,16]{2,1,0:T(8,128)} %param.7) | copy-start | bytes 3076
  6.5 104.9 %all-gather.3.cloned.1.call-start = ((), (), s32[]{:S(2)}) async-start(), calls=%async_computation.2 | async-start | bytes 9437184 | tf_op jit(solution)/shard_map/all_gather | solution.py:33
  19.2 32.6 %all-to-all-start = ((bf16[2,64,2048]{2,0,1:T(2,128)(2,1)}), bf16[2,64,2048]{2,0,1:T(2,128)(2,1)S(1)}, u32[]{:S(2)}, u32[]{:S(2)}) async-start(bf16[2,64,2048]{2,0,1:T(2,128)(2,1)} %broadcast_select_fusion), calls=%async_computation | async-start | bytes 1048576 | tf_op jit(solution)/shard_map/all_to_all | solution.py:29
  111.5 9.0 %copy-start.3 = (bf16[1,2048,2048]{2,1,0:T(8,128)(2,1)S(1)}, bf16[1,2048,2048]{2,1,0:T(8,128)(2,1)}, u32[]{:S(2)}) copy-start(bf16[1,2048,2048]{2,1,0:T(8,128)(2,1)} %all-gather.3.cloned.1.call-done) | copy-start | bytes 25165828
Sparse Core Ops, SparseCore 0:
  9.4 101.9 all-gather.2
where the time goes:
time: 164 us; the launch traced here: 163 us
  waiting for transfers between devices  77 us (47%)
  blocking collectives  28.5 us (17%)
  local copies, waits for them, and re-layouts  16.6 us (10%)
  starting transfers between devices  14.8 us (9%)
  between operations  13.6 us (8%)
  other arithmetic  7.06 us (4%)
  matrix products  5.67 us (3%)
    all_gather x1, waiting for transfers between devices, on_device(): lax.all_gather(block_rows, 'slab', axis=0, tiled=True)  59.5 us
    all_to_all x1, blocking collectives, on_device(): lax.all_to_all(product, 'pair', split_axis=1, concat_axis=1, tiled=True)  28.5 us
    all_to_all x1, waiting for transfers between devices, on_device(): lax.all_to_all(sorted_amps, 'pair', split_axis=1, concat_axis=1, tiled=True)  16.8 us
    all_to_all x1, starting transfers between devices, on_device(): lax.all_to_all(sorted_amps, 'pair', split_axis=1, concat_axis=1, tiled=True)  14.8 us
    mul x1, local copies, waits for them, and re-layouts, contract(): block_piece.reshape(rows_here, per_owner, tile_width)  8.96 us
    dot_general x1, matrix products, contract(): return jnp.dot(operand, masked, preferred_element_type=jnp.float32)  5.67 us
    sort x1, other arithmetic, on_device(): tile_order = jnp.argsort(owner, stable=True).reshape(n_pair, per_owner)  5.05 us
    gather x2, local copies, waits for them, and re-layouts, on_device(): jnp.take(amps, tile_order.reshape(-1), axis=1)  4.62 us
  transfers between devices with their start and end apart: 2, of which 2 were waited for; matrix products, arithmetic and copies ran while one was open for 8% of the time, Pallas kernels for 0%

commit v1 on v0

--- a/solution.py
+++ b/solution.py
@@ -30,7 +30,9 @@
     flat_rows = received.reshape(local_rows * n_pair, owner_span)
     summed = contract(
         flat_rows,
-        lax.all_gather(block_rows, "slab", axis=0, tiled=True),
+        jnp.concatenate(
+            lax.all_to_all(jnp.stack([block_rows] * lax.axis_size("slab")), "slab", 0, 0), axis=0
+        ),
         mask_rows,
         per_owner,
         tile_width,

time: 164 us -> 276 us (1.68)
  waiting for transfers between devices: 77 us -> 163 us
  blocking collectives: 28.5 us -> 55.3 us
  local copies, waits for them, and re-layouts: 16.6 us -> 35.2 us
  between operations: 13.6 us -> 0.14 us
  starting transfers between devices: 14.8 us -> 6.95 us
  other arithmetic: 7.06 us -> 13.9 us
  matrix products: 5.67 us -> 1.26 us
    all_to_all x1, waiting for transfers between devices: 16.8 us -> 163 us  [on_device(): lax.all_to_all(jnp.stack([block_rows] * lax.axis_size('slab')), 'slab', 0...]
    all_gather x1 -> x0, waiting for transfers between devices: 59.5 us -> none  [on_device(): lax.all_gather(block_rows, 'slab', axis=0, tiled=True)]
    all_to_all x0 -> x1, blocking collectives: none -> 32.4 us  [on_device(): lax.all_to_all(sorted_amps, 'pair', split_axis=1, concat_axis=1, tiled=True)]
    mul x1 -> x2, local copies, waits for them, and re-layouts: 8.96 us -> 23.2 us  [contract(): block_piece.reshape(rows_here, per_owner, tile_width)]
    all_to_all x1, starting transfers between devices: 14.8 us -> 6.95 us  [on_device(): lax.all_to_all(jnp.stack([block_rows] * lax.axis_size('slab')), 'slab', 0...]
    mul x0 -> x1, other arithmetic: none -> 7.52 us  [contract(): block_piece.reshape(rows_here, per_owner, tile_width)]
    all_to_all x1, blocking collectives: 28.5 us -> 23 us  [on_device(): lax.all_to_all(product, 'pair', split_axis=1, concat_axis=1, tiled=True)]
    dot_general x1, matrix products: 5.67 us -> 1.26 us  [contract(): return jnp.dot(operand, masked, preferred_element_type=jnp.float32)]
  transfers between devices with their start and end apart: 2 -> 1, of which waited for: 2 -> 1; matrix products, arithmetic and copies ran while one was open for 8% -> 9% of each run, Pallas kernels for 0% -> 0%
where the time goes in v1:
time: 276 us; the launch traced here: 275 us
  waiting for transfers between devices  163 us (59%)
  blocking collectives  55.3 us (20%)
  local copies, waits for them, and re-layouts  35.2 us (13%)
  other arithmetic  13.9 us (5%)
  starting transfers between devices  6.95 us (3%)
    all_to_all x1, waiting for transfers between devices, on_device(): lax.all_to_all(jnp.stack([block_rows] * lax.axis_size('slab')), 'slab', 0...  163 us
    all_to_all x1, blocking collectives, on_device(): lax.all_to_all(sorted_amps, 'pair', split_axis=1, concat_axis=1, tiled=True)  32.4 us
    mul x2, local copies, waits for them, and re-layouts, contract(): block_piece.reshape(rows_here, per_owner, tile_width)  23.2 us
    all_to_all x1, blocking collectives, on_device(): lax.all_to_all(product, 'pair', split_axis=1, concat_axis=1, tiled=True)  23 us
    mul x1, other arithmetic, contract(): block_piece.reshape(rows_here, per_owner, tile_width)  7.52 us
    all_to_all x1, starting transfers between devices, on_device(): lax.all_to_all(jnp.stack([block_rows] * lax.axis_size('slab')), 'slab', 0...  6.95 us
  transfers between devices with their start and end apart: 1, of which 1 were waited for; matrix products, arithmetic and copies ran while one was open for 9% of the time, Pallas kernels for 0%

profile of v1, /device:TPU:1, one launch (start us, length us, event | category | flops | bytes accessed | tf_op | source)
XLA Modules:
  0.0 275.4 jit_solution(8613421309607307584)
XLA Ops:
  0.0 0.0 copy-start
  0.0 0.0 copy-start.2
  0.0 5.2 %sort.17 = (s32[1024]{0:T(1024)}, s32[1024]{0:T(1024)S(1)}) sort(s32[1024]{0:T(1024)} %param.8, s32[1024]{0:T(1024)S(1)} %iota.4), dimensions={0}, to_apply=%region_0.0 | sort | flops 10240 | bytes 16384 | tf_op jit(solution)/shard_map/jit(argsort)/sort | solution.py:20
  5.2 0.0 copy-done
  5.2 4.4 %gather_fusion = bf16[1024,2,128]{2,0,1:T(8,128)(2,1)S(1)} fusion(bf16[2,1024,128]{2,1,0:T(8,128)(2,1)S(1)} %copy-done, s32[1024]{0:T(1024)S(1)} %fusion.1), kind=kCustom, calls=%fused_computation | custom fusion | bytes 1052672 | tf_op jit(solution)/shard_map/jit(_take)/gather | solution.py:21
  9.6 0.2 gather.13
  9.8 0.1 broadcast_in_dim.25
  9.9 0.2 broadcast_in_dim.26
  10.1 0.1 copy.16
  10.2 1.1 broadcast_select_fusion
  11.3 32.4 %all_to_all.15 = bf16[2,64,2048]{2,0,1:T(2,128)(2,1)S(1)} all-to-all(bf16[2,64,2048]{2,0,1:T(2,128)(2,1)S(1)} %broadcast_select_fusion), channel_id=1, replica_groups=mesh['pair'=64,'slab'=8] {'pair'}, dimensions={1} | all-to-all | bytes 1048576 | tf_op jit(solution)/shard_map/all_to_all | solution.py:29
  43.7 0.0 copy-done.2
  43.7 4.3 %stack.3 = bf16[8,256,2048]{2,1,0:T(8,128)(2,1)} broadcast(bf16[256,2048]{1,0:T(8,128)(2,1)S(1)} %bitcast.35), dimensions={1,2} | broadcast | bytes 9437184 | tf_op jit(solution)/shard_map/stack | solution.py:34
  47.9 0.0 copy-start.1
  47.9 0.0 copy-start.3
  47.9 7.0 %all-to-all-start.1 = ((bf16[8,256,2048]{2,1,0:T(8,128)(2,1)}), bf16[8,256,2048]{2,1,0:T(8,128)(2,1)}, u32[]{:S(2)}, u32[]{:S(2)}) async-start(bf16[8,256,2048]{2,1,0:T(8,128)(2,1)} %stack.3), calls=%async_computation.1 | async-start | bytes 16777216 | tf_op jit(solution)/shard_map/all_to_all | solution.py:34
  54.9 0.1 reshape.81
  55.0 0.0 copy-done.1
  55.0 0.6 gather_fusion.1
  55.7 0.0 copy-done.3
  55.7 0.1 fusion
  55.8 0.1 broadcast_in_dim.31
  55.8 9.9 %mul.17 = bf16[2048,16,128]{2,1,0:T(8,128)(2,1)} broadcast(bf16[2048,16]{1,0:T(8,128)(2,1)S(1)} %bitcast.33), dimensions={0,1} | broadcast | bytes 8454144 | tf_op jit(solution)/shard_map/mul | solution.py:10
  65.8 13.3 %mul.18 = bf16[8,256,2048]{2,1,0:T(8,128)(2,1)} reshape(bf16[2048,16,128]{2,1,0:T(8,128)(2,1)} %mul.17) | data formatting | bytes 16777216 | tf_op jit(solution)/shard_map/mul | solution.py:10
  79.1 0.2 copy.10
  79.3 162.7 %all-to-all-done.1 = bf16[8,256,2048]{2,1,0:T(8,128)(2,1)} async-done(((bf16[8,256,2048]{2,1,0:T(8,128)(2,1)}), bf16[8,256,2048]{2,1,0:T(8,128)(2,1)}, u32[]{:S(2)}, u32[]{:S(2)}) %all-to-all-start.1) | async-done | bytes 8388640 | tf_op jit(solution)/shard_map/all_to_all | solution.py:34
  242.0 7.5 %mul.19 = bf16[8,256,2048]{2,1,0:T(8,128)(2,1)S(1)} multiply(bf16[8,256,2048]{2,1,0:T(8,128)(2,1)} %all-to-all-done.1, bf16[8,256,2048]{2,1,0:T(8,128)(2,1)} %mul.18) | non-fusion elementwise | flops 4194304 | bytes 25165824 | tf_op jit(solution)/shard_map/mul | solution.py:10
  249.5 1.3 convolution_convert_fusion
  250.8 0.5 copy.11
  251.3 23.0 %all_to_all.16 = bf16[2,64,2048]{2,0,1:T(2,128)(2,1)S(1)} all-to-all(bf16[2,64,2048]{2,0,1:T(2,128)(2,1)S(1)} %copy.11), channel_id=1, replica_groups=mesh['pair'=64,'slab'=8] {'pair'}, dimensions={1} | all-to-all | bytes 1048576 | tf_op jit(solution)/shard_map/all_to_all | solution.py:41
  274.3 0.3 reshape.83
  274.6 0.8 copy.12
  (7 shorter events, 0.1 us)
Async XLA Ops:
  0.0 5.2 %copy-start = (bf16[2,1024,128]{2,1,0:T(8,128)(2,1)S(1)}, bf16[2,1024,128]{2,1,0:T(8,128)(2,1)}, u32[]{:S(2)}) copy-start(bf16[2,1024,128]{2,1,0:T(8,128)(2,1)} %param.5) | copy-start | bytes 1572868
  0.0 43.7 %copy-start.2 = (bf16[1,256,2048]{2,1,0:T(8,128)(2,1)S(1)}, bf16[1,256,2048]{2,1,0:T(8,128)(2,1)}, u32[]{:S(2)}) copy-start(bf16[1,256,2048]{2,1,0:T(8,128)(2,1)} %param.9) | copy-start | bytes 3145732
  47.9 7.1 %copy-start.1 = (s32[1024]{0:T(1024)S(1)}, s32[1024]{0:T(1024)}, u32[]{:S(2)}) copy-start(s32[1024]{0:T(1024)} %param.6) | copy-start | bytes 12292
  47.9 7.7 %copy-start.3 = (s32[1,16,16]{2,1,0:T(8,128)S(1)}, s32[1,16,16]{2,1,0:T(8,128)}, u32[]{:S(2)}) copy-start(s32[1,16,16]{2,1,0:T(8,128)} %param.7) | copy-start | bytes 3076
  47.9 194.0 %all-to-all-start.1 = ((bf16[8,256,2048]{2,1,0:T(8,128)(2,1)}), bf16[8,256,2048]{2,1,0:T(8,128)(2,1)}, u32[]{:S(2)}, u32[]{:S(2)}) async-start(bf16[8,256,2048]{2,1,0:T(8,128)(2,1)} %stack.3), calls=%async_computation.1 | async-start | bytes 16777216 | tf_op jit(solution)/shard_map/all_to_all | solution.py:34
